TPU v7x, 32 devices: a whole 2x2x4 slice. The times are simulated.
32 devices in a mesh: groups: 2 (over y), frame: 4 (over x, core), row: 4 (over z).
Axes of the slice: x: 2, y: 2, z: 4, core: 2. Of those that a mesh axis runs over, the one named last changes fastest.
Arguments:
- observed: float32 [16, 128, 2048], P('frame', ('groups', 'row')), parts along dimension 1, may hold values from 0.5 to 8
- kernels: float32 [8, 5], replicated, may hold values from 0.05 to 1
- band_kernel: int32 [16], P('groups'), parts along dimension 0, may hold values from 0 to 7
- masks: int32 [256, 128, 16], P(None, ('groups', 'row'), 'frame'), parts along dimension 1, may hold values from 0 to 1, as said below
Outputs:
- spikes: bfloat16 [16, 128, 2048], P(None, ('groups', 'row'), 'frame'), parts along dimension 1
- traces: float32 [512, 16], P(('groups', 'frame', 'row')), parts along dimension 0
There are 2 independent parts, one for each index of `groups`. A program takes and returns all parts, laid end to end along the dimension named above; an argument that names none is the same for every part. Nothing has to cross between parts.
Inputs may be any that keep to these rules, and one draw needn't show every extreme that they name: `masks`: each component covers the tile at its centre and a random half of the tiles within 8 rows and one tile column of that centre, so it covers at least one tile.
All inputs are finite; a program needn't handle non-finite values.
Results may differ from a plain program's by a relative error of at most 0.0062.
Values may be sent and summed in bfloat16 or wider, within the bound.
A program may use at most 64 MiB of HBM per device.

v0:
```python
import jax
import jax.numpy as jnp
from jax import lax
from jax.sharding import PartitionSpec as P

TILE = 128
BAND = 8
ITERS = 3


SMOOTHING = 1024.0
DECAY_RATE = 0.9


def padded_2(cells, sides, width):
    for axis, dim in sides:
        count = lax.axis_size(axis)
        ends = count - 1
        head = lax.slice_in_dim(cells, 0, width, axis=dim)
        tail = lax.slice_in_dim(cells, cells.shape[dim] - width, cells.shape[dim], axis=dim)
        cells = jnp.concatenate(
            [
                lax.ppermute(tail, axis, [(i, (i + 1) % count) for i in range(ends)]),
                cells,
                lax.ppermute(head, axis, [((i + 1) % count, i) for i in range(ends)]),
            ],
            axis=dim,
        )
    return cells


def tap_rows(tap_table, band_kernel, first_row, row_count, height):
    row_ids = jnp.clip(first_row + jnp.arange(row_count), 0, height - 1)
    row_bands = row_ids // BAND
    band_slots = jnp.arange(band_kernel.shape[0])
    kernel_ids = jnp.sum(
        jnp.where(row_bands[:, None] == band_slots[None, :], band_kernel[None, :], 0), axis=1
    )
    kernel_slots = jnp.arange(tap_table.shape[0])
    picked = jnp.where(
        kernel_ids[:, None, None] == kernel_slots[None, :, None], tap_table[None, :, :], 0.0
    )
    return jnp.sum(picked, axis=1)


def blur_rows(padded, row_taps, row_count):
    summed = row_taps[:, 0][None, :, None] * padded[:, 0:row_count]
    for offset in range(1, 5):
        summed = (
            summed + row_taps[:, offset][None, :, None] * padded[:, offset : offset + row_count]
        )
    return summed


def back_rows(padded_quotient, outer_taps, row_count):
    summed = outer_taps[4 : 4 + row_count, 0][None, :, None] * padded_quotient[:, 4 : 4 + row_count]
    for offset in range(1, 5):
        start = 4 - offset
        summed = (
            summed
            + outer_taps[start : start + row_count, offset][None, :, None]
            * padded_quotient[:, start : start + row_count]
        )
    return summed


def temporal(series_block):
    frame_total, item_count, columns = series_block.shape
    values = series_block.astype(jnp.float32).reshape(frame_total, item_count * columns)
    frame_ids = jnp.arange(frame_total)
    at_ends = (frame_ids == 0) | (frame_ids == frame_total - 1)
    middle = (1.0 + SMOOTHING * jnp.where(at_ends, 1.0, 2.0)).astype(jnp.float32)
    sub_diag = jnp.where(frame_ids == 0, 0.0, -SMOOTHING).astype(jnp.float32)
    super_diag = jnp.where(frame_ids == frame_total - 1, 0.0, -SMOOTHING).astype(jnp.float32)
    baseline = lax.linalg.tridiagonal_solve(sub_diag, middle, super_diag, values)
    detrended = values - baseline
    earlier = jnp.concatenate(
        [jnp.zeros((1, values.shape[1]), jnp.float32), detrended[:-1]], axis=0
    )
    result = (detrended - DECAY_RATE * earlier).astype(jnp.bfloat16)
    return result.reshape(frame_total, item_count, columns)


def local(observed, kernels, band_kernel, masks):
    frames_dev, rows_dev, row_pixels = observed.shape
    height = rows_dev * lax.axis_size("row")
    tap_table = kernels / jnp.sum(kernels, axis=1, keepdims=True)
    first_row = lax.axis_index("row") * rows_dev
    own_taps = tap_rows(tap_table, band_kernel, first_row, rows_dev, height)
    outer_taps = tap_rows(tap_table, band_kernel, first_row - 2, rows_dev + 4, height)
    current = observed
    for iteration in range(ITERS):
        padded = padded_2(current, (("row", 1),), 2)
        blurred = blur_rows(padded, own_taps, rows_dev)
        quotient = observed / blurred
        padded_quotient = padded_2(quotient, (("row", 1),), 2)
        current = current * back_rows(padded_quotient, outer_taps, rows_dev)
    estimate = current.astype(jnp.bfloat16)
    spikes = temporal(lax.all_to_all(estimate, "frame", split_axis=2, concat_axis=0, tiled=True))
    frames_all, _, columns = spikes.shape
    tile_count = columns // TILE
    tile_sums = jnp.sum(
        spikes.reshape(frames_all, rows_dev * tile_count, TILE).astype(jnp.float32), axis=2
    )
    weights = masks.astype(jnp.float32).reshape(masks.shape[0], rows_dev * tile_count)
    local_sums = lax.dot_general(
        weights, tile_sums, (((1,), (1,)), ((), ())), precision=lax.Precision.HIGHEST
    )
    counts = jnp.sum(weights, axis=1)
    trace_sums, totals = (
        lax.psum_scatter(local_sums, ("frame", "row"), scatter_dimension=0, tiled=True),
        lax.psum_scatter(counts, ("frame", "row"), scatter_dimension=0, tiled=True),
    )
    traces = trace_sums / (TILE * totals[:, None])
    return (spikes, traces)


def solution(mesh):
    in_specs = (
        P("frame", ("groups", "row"), None),
        P(),
        P("groups"),
        P(None, ("groups", "row"), "frame"),
    )
    out_specs = (P(None, ("groups", "row"), "frame"), P(("groups", "frame", "row"), None))
    return jax.shard_map(local, mesh=mesh, in_specs=in_specs, out_specs=out_specs, check_vma=False)
```

profile of v0, /device:TPU:0, one launch (start us, length us, event | category | flops | bytes accessed | tf_op | source)
XLA Modules:
  0.0 222.3 jit_solution(17117470301086755105)
XLA Ops:
  7.2 1.1 fusion.69
  8.4 5.0 %collective-permute-start = (f32[4,2,2048]{2,0,1:T(4,128)S(1)}, f32[4,2,2048]{2,0,1:T(4,128)S(1)}, u32[]{:S(2)}, u32[]{:S(2)}) collective-permute-start(f32[4,2,2048]{2,0,1:T(4,128)S(1)} %copy.150), channel_id=1, source_target_pairs={{0,1},{1,2},{2,3},{4,5},{5,6},{6,7},{8,9},{9,10},{10,11},{12,13},{... | collective-permute-start | bytes 196616 | tf_op jit(solution)/shard_map/ppermute | solution.py:23
  13.4 1.3 collective-permute-start.1
  14.7 0.8 reduce_sum.64
  15.5 0.8 broadcast_divide_fusion.1
  16.4 0.7 select_reduce_fusion.2
  17.2 0.7 select_reduce_fusion.3
  18.1 0.9 convert_element_type.45
  19.1 1.5 constant_dynamic-update-slice_fusion
  20.6 0.8 fusion.56
  21.4 1.3 collective-permute-start.2
  22.7 5.2 %collective-permute-start.3 = (f32[4,2,2048]{2,0,1:T(4,128)S(1)}, f32[4,2,2048]{2,0,1:T(4,128)S(1)}, u32[]{:S(2)}, u32[]{:S(2)}) collective-permute-start(f32[4,2,2048]{2,0,1:T(4,128)S(1)} %get-tuple-element.75), channel_id=1, source_target_pairs={{0,1},{1,2},{2,3},{4,5},{5,6},{6,7},{8,9},{9,10},{10,11},{12,13},{... | collective-permute-start | bytes 196616 | tf_op jit(solution)/shard_map/ppermute | solution.py:23
  28.2 1.6 collective-permute-done.3
  29.8 0.9 fusion.40
  30.7 4.3 %collective-permute-start.4 = (f32[4,2,2048]{2,0,1:T(4,128)S(1)}, f32[4,2,2048]{2,0,1:T(4,128)S(1)}, u32[]{:S(2)}, u32[]{:S(2)}) collective-permute-start(f32[4,2,2048]{2,0,1:T(4,128)S(1)} %get-tuple-element.72), channel_id=1, source_target_pairs={{0,1},{1,2},{2,3},{4,5},{5,6},{6,7},{8,9},{9,10},{10,11},{12,13},{... | collective-permute-start | bytes 196616 | tf_op jit(solution)/shard_map/ppermute | solution.py:23
  34.9 1.3 collective-permute-start.5
  36.2 0.7 fusion.71
  37.0 4.1 %collective-permute-done.5 = f32[4,2,2048]{2,0,1:T(4,128)S(1)} collective-permute-done((f32[4,2,2048]{2,0,1:T(4,128)S(1)}, f32[4,2,2048]{2,0,1:T(4,128)S(1)}, u32[]{:S(2)}, u32[]{:S(2)}) %collective-permute-start.5) | collective-permute-done | bytes 65568 | tf_op jit(solution)/shard_map/ppermute | solution.py:25
  41.1 0.9 fusion.31
  42.0 1.3 collective-permute-start.6
  43.3 4.5 %collective-permute-start.7 = (f32[4,2,2048]{2,0,1:T(4,128)S(1)}, f32[4,2,2048]{2,0,1:T(4,128)S(1)}, u32[]{:S(2)}, u32[]{:S(2)}) collective-permute-start(f32[4,2,2048]{2,0,1:T(4,128)S(1)} %get-tuple-element.71), channel_id=1, source_target_pairs={{0,1},{1,2},{2,3},{4,5},{5,6},{6,7},{8,9},{9,10},{10,11},{12,13},{... | collective-permute-start | bytes 196616 | tf_op jit(solution)/shard_map/ppermute | solution.py:23
  48.2 1.6 collective-permute-done.7
  49.8 0.6 fusion.22
  50.4 4.3 %collective-permute-start.8 = (f32[4,2,2048]{2,0,1:T(4,128)S(1)}, f32[4,2,2048]{2,0,1:T(4,128)S(1)}, u32[]{:S(2)}, u32[]{:S(2)}) collective-permute-start(f32[4,2,2048]{2,0,1:T(4,128)S(1)} %get-tuple-element.68), channel_id=1, source_target_pairs={{0,1},{1,2},{2,3},{4,5},{5,6},{6,7},{8,9},{9,10},{10,11},{12,13},{... | collective-permute-start | bytes 196616 | tf_op jit(solution)/shard_map/ppermute | solution.py:23
  54.7 1.3 collective-permute-start.9
  56.0 0.7 fusion.72
  58.0 3.5 %collective-permute-done.9 = f32[4,2,2048]{2,0,1:T(4,128)S(1)} collective-permute-done((f32[4,2,2048]{2,0,1:T(4,128)S(1)}, f32[4,2,2048]{2,0,1:T(4,128)S(1)}, u32[]{:S(2)}, u32[]{:S(2)}) %collective-permute-start.9) | collective-permute-done | bytes 65568 | tf_op jit(solution)/shard_map/ppermute | solution.py:25
  61.5 0.9 fusion.13
  62.4 1.3 collective-permute-start.10
  63.7 4.5 %collective-permute-start.11 = (f32[4,2,2048]{2,0,1:T(4,128)S(1)}, f32[4,2,2048]{2,0,1:T(4,128)S(1)}, u32[]{:S(2)}, u32[]{:S(2)}) collective-permute-start(f32[4,2,2048]{2,0,1:T(4,128)S(1)} %get-tuple-element.67), channel_id=1, source_target_pairs={{0,1},{1,2},{2,3},{4,5},{5,6},{6,7},{8,9},{9,10},{10,11},{12,13},{... | collective-permute-start | bytes 196616 | tf_op jit(solution)/shard_map/ppermute | solution.py:23
  68.5 1.6 collective-permute-done.11
  70.1 0.6 fusion.60
  70.7 1.5 copy.117
  72.2 2.9 %reshape.1472 = bf16[4,2,16384]{2,1,0:T(2,128)(2,1)} reshape(bf16[2048,4,16]{2,1,0:T(4,128)(2,1)S(1)} %bitcast.135) | data formatting | bytes 524288
  75.1 3.4 %all-to-all-start = ((bf16[4,2,16384]{2,1,0:T(2,128)(2,1)}), bf16[4,2,16384]{2,1,0:T(2,128)(2,1)S(1)}, u32[]{:S(2)}, u32[]{:S(2)}) async-start(bf16[4,2,16384]{2,1,0:T(2,128)(2,1)} %reshape.1472), calls=%async_computation | async-start | bytes 524288 | tf_op jit(solution)/shard_map/all_to_all | solution.py:99
  78.6 0.7 fusion.70
  108.1 35.6 %all-reduce.1 = f32[256]{0:T(256)S(1)} all-reduce(f32[256]{0:T(256)S(1)} %convert_reduce_fusion), channel_id=3, replica_groups=mesh['groups'=2,'frame'=4,'row'=4] {'frame','row'}, use_global_device_ids=true, to_apply=%region_8.9.clone | all-reduce | flops 256 | bytes 2048
  143.7 1.4 reshape.1473
  145.1 1.1 copy.118
  146.9 0.7 slice_bitcast_fusion
  148.6 9.3 %subtract_divide_fusion.1 = (f32[1,8192]{1,0:T(1,128)S(1)}, f32[1,8192]{1,0:T(1,128)S(1)}, f32[1,8192]{1,0:T(1,128)S(1)}, f32[1,8192]{1,0:T(1,128)S(1)}, f32[1,8...) fusion(f32[1,8192]{1,0:T(1,128)S(1)} %bitcast.161, ...), kind=kLoop, calls=%fused_computation.131 | loop fusion | flops 344064 | bytes 950384 | tf_op jit(solution)/shard_map/eval_jaxpr/div | solution.py:75
  157.9 1.0 multiply_subtract_fusion
  158.9 0.8 concatenate.72
  160.3 0.7 copy.122
  161.1 0.8 copy.141
  161.9 52.1 %reduce-scatter.4.cloned.1.call-done = f32[16,16]{1,0:T(8,128)} async-done(((f32[256,16]{1,0:T(8,128)}), f32[16,16]{1,0:T(8,128)}) %reduce-scatter.4.cloned.1.call-update) | async-done | bytes 1040
  214.0 0.8 copy.123
  214.8 0.7 copy.121
  (66 shorter events, 4.3 us)
Async XLA Ops:
  7.2 13.4 %copy-start = (f32[4,16,2048]{2,1,0:T(8,128)S(1)}, f32[4,16,2048]{2,1,0:T(8,128)}, u32[]{:S(2)}) copy-start(f32[4,16,2048]{2,1,0:T(8,128)} %param.4) | copy-start | bytes 1572868
  8.4 10.7 %collective-permute-start = (f32[4,2,2048]{2,0,1:T(4,128)S(1)}, f32[4,2,2048]{2,0,1:T(4,128)S(1)}, u32[]{:S(2)}, u32[]{:S(2)}) collective-permute-start(f32[4,2,2048]{2,0,1:T(4,128)S(1)} %copy.150), channel_id=1, source_target_pairs={{0,1},{1,2},{2,3},{4,5},{5,6},{6,7},{8,9},{9,10},{10,11},{12,13},{... | collective-permute-start | bytes 196616 | tf_op jit(solution)/shard_map/ppermute | solution.py:23
  13.4 7.2 %collective-permute-start.1 = (f32[4,2,2048]{2,0,1:T(4,128)S(1)}, f32[4,2,2048]{2,0,1:T(4,128)S(1)}, u32[]{:S(2)}, u32[]{:S(2)}) collective-permute-start(f32[4,2,2048]{2,0,1:T(4,128)S(1)} %copy.149), channel_id=1, source_target_pairs={{1,0},{2,1},{3,2},{5,4},{6,5},{7,6},{9,8},{10,9},{11,10},{13,12},{... | collective-permute-start | bytes 196616 | tf_op jit(solution)/shard_map/ppermute | solution.py:25
  21.4 6.8 %collective-permute-start.2 = (f32[4,2,2048]{2,0,1:T(4,128)S(1)}, f32[4,2,2048]{2,0,1:T(4,128)S(1)}, u32[]{:S(2)}, u32[]{:S(2)}) collective-permute-start(f32[4,2,2048]{2,0,1:T(4,128)S(1)} %get-tuple-element.74), channel_id=1, source_target_pairs={{1,0},{2,1},{3,2},{5,4},{6,5},{7,6},{9,8},{10,9},{11,10},{13,12},{... | collective-permute-start | bytes 196616 | tf_op jit(solution)/shard_map/ppermute | solution.py:25
  22.7 7.1 %collective-permute-start.3 = (f32[4,2,2048]{2,0,1:T(4,128)S(1)}, f32[4,2,2048]{2,0,1:T(4,128)S(1)}, u32[]{:S(2)}, u32[]{:S(2)}) collective-permute-start(f32[4,2,2048]{2,0,1:T(4,128)S(1)} %get-tuple-element.75), channel_id=1, source_target_pairs={{0,1},{1,2},{2,3},{4,5},{5,6},{6,7},{8,9},{9,10},{10,11},{12,13},{... | collective-permute-start | bytes 196616 | tf_op jit(solution)/shard_map/ppermute | solution.py:23
  30.7 6.3 %collective-permute-start.4 = (f32[4,2,2048]{2,0,1:T(4,128)S(1)}, f32[4,2,2048]{2,0,1:T(4,128)S(1)}, u32[]{:S(2)}, u32[]{:S(2)}) collective-permute-start(f32[4,2,2048]{2,0,1:T(4,128)S(1)} %get-tuple-element.72), channel_id=1, source_target_pairs={{0,1},{1,2},{2,3},{4,5},{5,6},{6,7},{8,9},{9,10},{10,11},{12,13},{... | collective-permute-start | bytes 196616 | tf_op jit(solution)/shard_map/ppermute | solution.py:23
  34.9 6.2 %collective-permute-start.5 = (f32[4,2,2048]{2,0,1:T(4,128)S(1)}, f32[4,2,2048]{2,0,1:T(4,128)S(1)}, u32[]{:S(2)}, u32[]{:S(2)}) collective-permute-start(f32[4,2,2048]{2,0,1:T(4,128)S(1)} %get-tuple-element.73), channel_id=1, source_target_pairs={{1,0},{2,1},{3,2},{5,4},{6,5},{7,6},{9,8},{10,9},{11,10},{13,12},{... | collective-permute-start | bytes 196616 | tf_op jit(solution)/shard_map/ppermute | solution.py:25
  42.0 6.2 %collective-permute-start.6 = (f32[4,2,2048]{2,0,1:T(4,128)S(1)}, f32[4,2,2048]{2,0,1:T(4,128)S(1)}, u32[]{:S(2)}, u32[]{:S(2)}) collective-permute-start(f32[4,2,2048]{2,0,1:T(4,128)S(1)} %get-tuple-element.70), channel_id=1, source_target_pairs={{1,0},{2,1},{3,2},{5,4},{6,5},{7,6},{9,8},{10,9},{11,10},{13,12},{... | collective-permute-start | bytes 196616 | tf_op jit(solution)/shard_map/ppermute | solution.py:25
  43.3 6.4 %collective-permute-start.7 = (f32[4,2,2048]{2,0,1:T(4,128)S(1)}, f32[4,2,2048]{2,0,1:T(4,128)S(1)}, u32[]{:S(2)}, u32[]{:S(2)}) collective-permute-start(f32[4,2,2048]{2,0,1:T(4,128)S(1)} %get-tuple-element.71), channel_id=1, source_target_pairs={{0,1},{1,2},{2,3},{4,5},{5,6},{6,7},{8,9},{9,10},{10,11},{12,13},{... | collective-permute-start | bytes 196616 | tf_op jit(solution)/shard_map/ppermute | solution.py:23
  50.4 7.6 %collective-permute-start.8 = (f32[4,2,2048]{2,0,1:T(4,128)S(1)}, f32[4,2,2048]{2,0,1:T(4,128)S(1)}, u32[]{:S(2)}, u32[]{:S(2)}) collective-permute-start(f32[4,2,2048]{2,0,1:T(4,128)S(1)} %get-tuple-element.68), channel_id=1, source_target_pairs={{0,1},{1,2},{2,3},{4,5},{5,6},{6,7},{8,9},{9,10},{10,11},{12,13},{... | collective-permute-start | bytes 196616 | tf_op jit(solution)/shard_map/ppermute | solution.py:23
  54.7 6.8 %collective-permute-start.9 = (f32[4,2,2048]{2,0,1:T(4,128)S(1)}, f32[4,2,2048]{2,0,1:T(4,128)S(1)}, u32[]{:S(2)}, u32[]{:S(2)}) collective-permute-start(f32[4,2,2048]{2,0,1:T(4,128)S(1)} %get-tuple-element.69), channel_id=1, source_target_pairs={{1,0},{2,1},{3,2},{5,4},{6,5},{7,6},{9,8},{10,9},{11,10},{13,12},{... | collective-permute-start | bytes 196616 | tf_op jit(solution)/shard_map/ppermute | solution.py:25
  62.4 6.2 %collective-permute-start.10 = (f32[4,2,2048]{2,0,1:T(4,128)S(1)}, f32[4,2,2048]{2,0,1:T(4,128)S(1)}, u32[]{:S(2)}, u32[]{:S(2)}) collective-permute-start(f32[4,2,2048]{2,0,1:T(4,128)S(1)} %get-tuple-element.66), channel_id=1, source_target_pairs={{1,0},{2,1},{3,2},{5,4},{6,5},{7,6},{9,8},{10,9},{11,10},{13,12},{... | collective-permute-start | bytes 196616 | tf_op jit(solution)/shard_map/ppermute | solution.py:25
  63.7 6.4 %collective-permute-start.11 = (f32[4,2,2048]{2,0,1:T(4,128)S(1)}, f32[4,2,2048]{2,0,1:T(4,128)S(1)}, u32[]{:S(2)}, u32[]{:S(2)}) collective-permute-start(f32[4,2,2048]{2,0,1:T(4,128)S(1)} %get-tuple-element.67), channel_id=1, source_target_pairs={{0,1},{1,2},{2,3},{4,5},{5,6},{6,7},{8,9},{9,10},{10,11},{12,13},{... | collective-permute-start | bytes 196616 | tf_op jit(solution)/shard_map/ppermute | solution.py:23
  72.2 34.6 %copy-start.2 = (u32[32]{0:T(128)S(1)}, u32[32]{0:T(128)}, u32[]{:S(2)}) copy-start(u32[32]{0:T(128)} %constant.60) | copy-start | bytes 388
  72.2 35.9 %copy-start.1 = (s32[256,16,4]{0,2,1:T(4,128)S(1)}, s32[256,16,4]{0,2,1:T(4,128)}, u32[]{:S(2)}) copy-start(s32[256,16,4]{0,2,1:T(4,128)} %param.7) | copy-start | bytes 196612
  75.1 68.6 %all-to-all-start = ((bf16[4,2,16384]{2,1,0:T(2,128)(2,1)}), bf16[4,2,16384]{2,1,0:T(2,128)(2,1)S(1)}, u32[]{:S(2)}, u32[]{:S(2)}) async-start(bf16[4,2,16384]{2,1,0:T(2,128)(2,1)} %reshape.1472), calls=%async_computation | async-start | bytes 524288 | tf_op jit(solution)/shard_map/all_to_all | solution.py:99
  78.5 135.5 %reduce-scatter.4.cloned.1.call-start = ((), (), s32[]{:S(2)}) async-start(), calls=%async_computation.2 | async-start | bytes 139264
Sparse Core Ops, SparseCore 0:
  161.2 52.7 reduce-scatter.3
where the time goes:
time: 224 us; the launch traced here: 222 us
  waiting for transfers between devices  65.4 us (29%)
  between operations  44.1 us (20%)
  starting transfers between devices  39 us (17%)
  blocking collectives  35.6 us (16%)
  other arithmetic  20.2 us (9%)
  local copies, waits for them, and re-layouts  18 us (8%)
    unnamed x2, waiting for transfers between devices  52.1 us
    unnamed x1, blocking collectives  35.6 us
    ppermute x6, starting transfers between devices, padded_2(): lax.ppermute(tail, axis, [(i, (i + 1) % count) for i in range(ends)])  27.8 us
    div x1, other arithmetic, temporal(): lax.linalg.tridiagonal_solve(sub_diag, middle, super_diag, values)  9.26 us
    unnamed x34, local copies, waits for them, and re-layouts  8.98 us
    ppermute x6, waiting for transfers between devices, padded_2(): lax.ppermute(head, axis, [((i + 1) % count, i) for i in range(ends)])  8.5 us
    ppermute x6, starting transfers between devices, padded_2(): lax.ppermute(head, axis, [((i + 1) % count, i) for i in range(ends)])  7.75 us
    ppermute x6, waiting for transfers between devices, padded_2(): lax.ppermute(tail, axis, [(i, (i + 1) % count) for i in range(ends)])  4.75 us
  transfers between devices with their start and end apart: 14, of which 9 were waited for; matrix products, arithmetic and copies ran while one was open for 4% of the time, Pallas kernels for 0%

commit v1 on v0

v1 whole, which is shorter than its diff:
```python
import functools
import jax
import jax.numpy as jnp
from jax import lax
from jax.experimental import pallas as pl
from jax.experimental.pallas import tpu as pltpu
from jax.sharding import PartitionSpec as P

TILE = 128
BAND = 8
ITERS = 3
REACH = 2
HALO = 2 * REACH * ITERS
OWN = 16

SMOOTHING = 1024.0
DECAY_RATE = 0.9


def thomas_factors(frames):
    inverse, upper = [], []
    for t in range(frames):
        diag = 1.0 + SMOOTHING * (1.0 if t in (0, frames - 1) else 2.0)
        pivot = diag if t == 0 else diag + SMOOTHING * upper[-1]
        inverse.append(1.0 / pivot)
        upper.append(-SMOOTHING / pivot)
    return inverse, upper


def body(cfg, obs_hbm, kern_ref, band_ref, masks_hbm, spikes_ref, traces_ref,
         obs, cur, quo, taps, outm, send, est, masks, wide, wt, rhs, part, gath,
         load_sem, mask_sem, zs, zr, fs, fr, rs, rr):
    nf, nr, fd, rows, cpd, comps = cfg
    ct_n = cpd // TILE
    frames = fd * nf
    nd = nf * nr
    brows = rows + 2 * OWN
    slot = rhs_slot(frames)
    pack = TILE // slot
    kdev = comps // nd
    kq = kdev // pack
    f = lax.axis_index("frame")
    r = lax.axis_index("row")
    me = f * nr + r

    def chunk_of(s):
        dx = s // 2 + 1
        return ((f // 2 + dx) % (nf // 2)) * 2 + (f % 2 + 1 + s) % 2

    def load(s, ct):
        col = pl.multiple_of(chunk_of(s) * cpd + ct * TILE, TILE)
        return pltpu.make_async_copy(
            obs_hbm.at[:, :, pl.ds(col, TILE)],
            obs.at[s, :, ct, OWN : OWN + rows, :],
            load_sem.at[s, ct],
        )

    def up(s):
        return pltpu.make_async_remote_copy(
            src_ref=obs.at[s, :, :, OWN : OWN + HALO, :],
            dst_ref=obs.at[s, :, :, OWN + rows : OWN + rows + HALO, :],
            send_sem=zs.at[0, s],
            recv_sem=zr.at[0, s],
            device_id={"row": r - 1},
            device_id_type=pl.DeviceIdType.MESH,
        )

    def down(s):
        return pltpu.make_async_remote_copy(
            src_ref=obs.at[s, :, :, OWN + rows - HALO : OWN + rows, :],
            dst_ref=obs.at[s, :, :, OWN - HALO : OWN, :],
            send_sem=zs.at[1, s],
            recv_sem=zr.at[1, s],
            device_id={"row": r + 1},
            device_id_type=pl.DeviceIdType.MESH,
        )

    def frame_copy(s):
        c = chunk_of(s)
        return pltpu.make_async_remote_copy(
            src_ref=send.at[s],
            dst_ref=est.at[f],
            send_sem=fs.at[s],
            recv_sem=fr.at[f],
            device_id={"frame": c},
            device_id_type=pl.DeviceIdType.MESH,
        )

    def frame_wait(s):
        c = chunk_of(s)
        return pltpu.make_async_remote_copy(
            src_ref=send.at[s],
            dst_ref=est.at[c],
            send_sem=fs.at[s],
            recv_sem=fr.at[c],
            device_id={"frame": c},
            device_id_type=pl.DeviceIdType.MESH,
        )

    def part_copy(off):
        d = (me + off) % nd
        return pltpu.make_async_remote_copy(
            src_ref=part.at[d],
            dst_ref=gath.at[me],
            send_sem=rs.at[d],
            recv_sem=rr.at[me],
            device_id={"frame": d // nr, "row": d % nr},
            device_id_type=pl.DeviceIdType.MESH,
        )

    def part_wait(off):
        d = (me + off) % nd
        return pltpu.make_async_remote_copy(
            src_ref=part.at[d],
            dst_ref=gath.at[d],
            send_sem=rs.at[d],
            recv_sem=rr.at[d],
            device_id={"frame": d // nr, "row": d % nr},
            device_id_type=pl.DeviceIdType.MESH,
        )

    barrier = pltpu.get_barrier_semaphore()

    def greet(off, _):
        d = (me + off) % nd
        pl.semaphore_signal(
            barrier, inc=1, device_id={"frame": d // nr, "row": d % nr},
            device_id_type=pl.DeviceIdType.MESH,
        )
        return 0

    lax.fori_loop(1, nd, greet, 0)

    def start_loads(s, _):
        for ct in range(ct_n):
            load(s, ct).start()
        return 0

    lax.fori_loop(0, nf, start_loads, 0)
    mask_copy = pltpu.make_async_copy(masks_hbm, masks, mask_sem)
    mask_copy.start()

    bands = band_ref.shape[0]
    for b in range(brows // BAND):
        band = r * (rows // BAND) - OWN // BAND + b
        inside = jnp.where((band >= 0) & (band < bands), 1.0, 0.0).astype(jnp.float32)
        kid = band_ref[jnp.clip(band, 0, bands - 1)]
        row_taps = [jnp.full((BAND, TILE), kern_ref[kid, j], jnp.float32) for j in range(5)]
        total = row_taps[0] + row_taps[1] + row_taps[2] + row_taps[3] + row_taps[4]
        for j in range(5):
            taps[j, b * BAND : (b + 1) * BAND, :] = row_taps[j] / total * inside
        outm[b * BAND : (b + 1) * BAND, :] = jnp.full((BAND, TILE), 1.0 - inside, jnp.float32)

    pl.semaphore_wait(barrier, nd - 1)

    def start_halo(s, _):
        for ct in range(ct_n):
            load(s, ct).wait()

        @pl.when(r > 0)
        def _():
            up(s).start()

        @pl.when(r < nr - 1)
        def _():
            down(s).start()

        return 0

    lax.fori_loop(0, nf, start_halo, 0)

    @pl.when(r == 0)
    def _():
        def clear(s, _):
            obs[s, :, :, OWN - HALO : OWN, :] = jnp.zeros((fd, ct_n, HALO, TILE), jnp.float32)
            return 0
        lax.fori_loop(0, nf, clear, 0)

    @pl.when(r == nr - 1)
    def _():
        def clear(s, _):
            obs[s, :, :, OWN + rows : OWN + rows + HALO, :] = jnp.zeros((fd, ct_n, HALO, TILE), jnp.float32)
            return 0
        lax.fori_loop(0, nf, clear, 0)

    mask_copy.wait()
    wide[...] = jnp.zeros_like(wide)
    for h in range(rows):
        wide[h * ct_n : (h + 1) * ct_n, :] = masks[h].astype(jnp.float32)
    wt[...] = jnp.transpose(wide[...])
    rhs[...] = jnp.zeros_like(rhs)
    for m in range(pack):
        rhs[m, m * slot + frames : m * slot + frames + 1, :] = jnp.ones((1, TILE), jnp.float32)

    def restore(s, ff, store):
        for it in range(ITERS):
            source = obs.at[s, ff] if it == 0 else cur.at[ff]
            reach = HALO - 2 * REACH * it
            lo = OWN - reach + REACH
            hi = OWN + rows + reach - REACH
            for a in range(lo, hi, 8):
                blurred = outm[a : a + 8, :][None] + taps[0, a : a + 8, :][None] * source[:, pl.ds(a - 2, 8), :]
                for j in range(1, 5):
                    blurred = blurred + taps[j, a : a + 8, :][None] * source[:, pl.ds(a + j - 2, 8), :]
                quo[ff, :, pl.ds(a, 8), :] = obs[s, ff, :, pl.ds(a, 8), :] / blurred
            last = it == ITERS - 1
            lo, hi = lo + REACH, hi - REACH
            step = hi - lo if last else 8
            for a in range(lo, hi, step):
                back = None
                for j in range(5):
                    at = a + 2 - j
                    term = taps[j, at : at + step, :][None] * quo[ff, :, pl.ds(at, step), :]
                    back = term if back is None else back + term
                value = source[:, pl.ds(a, step), :] * back
                if last:
                    store(value.astype(jnp.bfloat16))
                else:
                    cur[ff, :, pl.ds(a, step), :] = value

    def wait_halo(s):
        @pl.when(r > 0)
        def _():
            down(s).wait_recv()

        @pl.when(r < nr - 1)
        def _():
            up(s).wait_recv()

    def remote_chunk(s, _):
        wait_halo(s)

        def one(ff, _):
            def store(value):
                for ct in range(ct_n):
                    send[s, ff, :, ct * TILE : (ct + 1) * TILE] = value[ct]
            restore(s, ff, store)
            return 0

        lax.fori_loop(0, fd, one, 0)
        frame_copy(s).start()
        return 0

    lax.fori_loop(0, nf - 1, remote_chunk, 0)
    own = nf - 1
    wait_halo(own)

    def one(ff, _):
        def store(value):
            for ct in range(ct_n):
                est[f, ff, :, ct * TILE : (ct + 1) * TILE] = value[ct]
        restore(own, ff, store)
        return 0

    lax.fori_loop(0, fd, one, 0)

    def frame_recv(s, _):
        frame_wait(s).wait_recv()
        return 0

    lax.fori_loop(0, nf - 1, frame_recv, 0)

    inverse, upper = thomas_factors(frames)
    for ct in range(ct_n):
        cols = slice(ct * TILE, (ct + 1) * TILE)
        value = [est[t // fd, t % fd, :, cols].astype(jnp.float32) for t in range(frames)]
        swept = []
        for t in range(frames):
            right = value[t] if t == 0 else value[t] + SMOOTHING * swept[-1]
            swept.append(right * inverse[t])
        base = [None] * frames
        for t in reversed(range(frames)):
            base[t] = swept[t] if t == frames - 1 else swept[t] - upper[t] * base[t + 1]
        earlier = None
        for t in range(frames):
            detrended = value[t] - base[t]
            out = detrended if t == 0 else detrended - DECAY_RATE * earlier
            spikes_ref[t, :, cols] = out.astype(jnp.bfloat16)
            earlier = detrended

    pixel_tile = lax.broadcasted_iota(jnp.int32, (cpd, TILE), 0) // TILE
    lane = lax.broadcasted_iota(jnp.int32, (cpd, TILE), 1)
    picks = jnp.where(pixel_tile == lane % ct_n, 1.0, 0.0).astype(jnp.bfloat16)
    sums = jnp.dot(
        spikes_ref[...].reshape(frames * rows, cpd), picks, preferred_element_type=jnp.float32
    ).reshape(frames, rows, TILE)
    row_id = lax.broadcasted_iota(jnp.int32, (rows, TILE), 0)
    row_lane = lax.broadcasted_iota(jnp.int32, (rows, TILE), 1)
    tile_sums = jnp.sum(jnp.where((row_id == row_lane // ct_n)[None], sums, 0.0), axis=1)
    total = None
    for m in range(pack):
        rhs[m, m * slot : m * slot + frames, :] = tile_sums
        left = wt[pl.ds(m, comps // pack, stride=pack), :] if pack > 1 else wt[...]
        term = lax.dot_general(
            left, rhs[m], (((1,), (1,)), ((), ())),
            precision=lax.Precision.HIGHEST, preferred_element_type=jnp.float32,
        )
        total = term if total is None else total + term
    for d in range(nd):
        part[d] = total[d * kq : (d + 1) * kq, :]

    def send_part(off, _):
        part_copy(off).start()
        return 0

    lax.fori_loop(1, nd, send_part, 0)
    gath[me] = part[me]

    def recv_part(off, _):
        part_wait(off).wait_recv()
        return 0

    lax.fori_loop(1, nd, recv_part, 0)
    summed = jnp.sum(gath[...], axis=0)
    for m in range(pack):
        piece = summed[:, m * slot : m * slot + frames]
        count = summed[:, m * slot + frames : m * slot + frames + 1]
        answer = piece / (TILE * count)
        for q in range(kq):
            traces_ref[q * pack + m : q * pack + m + 1, :] = answer[q : q + 1, :]

    def drain(s, _):
        frame_copy(s).wait_send()
        return 0

    lax.fori_loop(0, nf - 1, drain, 0)

    def drain_halo(s, _):
        @pl.when(r > 0)
        def _():
            up(s).wait_send()

        @pl.when(r < nr - 1)
        def _():
            down(s).wait_send()

        return 0

    lax.fori_loop(0, nf, drain_halo, 0)

    def drain_part(off, _):
        part_copy(off).wait_send()
        return 0

    lax.fori_loop(1, nd, drain_part, 0)


def rhs_slot(frames):
    slot = 32
    while slot < frames + 1:
        slot *= 2
    return slot


def local(observed, kernels, band_kernel, masks):
    fd, rows, width = observed.shape
    nf = lax.axis_size("frame")
    nr = lax.axis_size("row")
    frames = fd * nf
    cpd = width // nf
    ct_n = cpd // TILE
    comps = masks.shape[0]
    nd = nf * nr
    brows = rows + 2 * OWN
    slot = rhs_slot(frames)
    pack = TILE // slot
    kdev = comps // nd
    f32, bf16 = jnp.float32, jnp.bfloat16
    dma = pltpu.SemaphoreType.DMA
    return pl.pallas_call(
        functools.partial(body, (nf, nr, fd, rows, cpd, comps)),
        out_shape=(
            jax.ShapeDtypeStruct((frames, rows, cpd), bf16),
            jax.ShapeDtypeStruct((kdev, frames), f32),
        ),
        in_specs=[
            pl.BlockSpec(memory_space=pl.ANY),
            pl.BlockSpec(memory_space=pltpu.SMEM),
            pl.BlockSpec(memory_space=pltpu.SMEM),
            pl.BlockSpec(memory_space=pl.ANY),
        ],
        out_specs=(
            pl.BlockSpec(memory_space=pltpu.VMEM),
            pl.BlockSpec(memory_space=pltpu.VMEM),
        ),
        scratch_shapes=[
            pltpu.VMEM((nf, fd, ct_n, brows, TILE), f32),
            pltpu.VMEM((fd, ct_n, brows, TILE), f32),
            pltpu.VMEM((fd, ct_n, brows, TILE), f32),
            pltpu.VMEM((5, brows, TILE), f32),
            pltpu.VMEM((brows, TILE), f32),
            pltpu.VMEM((nf, fd, rows, cpd), bf16),
            pltpu.VMEM((nf, fd, rows, cpd), bf16),
            pltpu.VMEM((rows, ct_n, comps), jnp.int32),
            pltpu.VMEM((TILE, comps), f32),
            pltpu.VMEM((comps, TILE), f32),
            pltpu.VMEM((pack, TILE, TILE), f32),
            pltpu.VMEM((nd, kdev // pack, TILE), f32),
            pltpu.VMEM((nd, kdev // pack, TILE), f32),
            dma((nf, ct_n)),
            dma,
            dma((2, nf)),
            dma((2, nf)),
            dma((nf,)),
            dma((nf,)),
            dma((nd,)),
            dma((nd,)),
        ],
        compiler_params=pltpu.CompilerParams(collective_id=0, has_side_effects=True),
        name="restore_all",
    )(observed, kernels, band_kernel, jnp.transpose(masks, (1, 2, 0)))


def solution(mesh):
    in_specs = (
        P("frame", ("groups", "row"), None),
        P(),
        P("groups"),
        P(None, ("groups", "row"), "frame"),
    )
    out_specs = (P(None, ("groups", "row"), "frame"), P(("groups", "frame", "row"), None))
    return jax.shard_map(local, mesh=mesh, in_specs=in_specs, out_specs=out_specs, check_vma=False)
```

time: 224 us -> 26.8 us (0.12)
  waiting for transfers between devices: 65.4 us -> 0 us
  between operations: 44.1 us -> 0.65 us
  starting transfers between devices: 39 us -> 0 us
  blocking collectives: 35.6 us -> 0 us
  Pallas kernels: 0 us -> 23.7 us
  other arithmetic: 20.2 us -> 0 us
  local copies, waits for them, and re-layouts: 18 us -> 2.28 us
    unnamed x2 -> x0, waiting for transfers between devices: 52.1 us -> none
    unnamed x1 -> x0, blocking collectives: 35.6 us -> none
    ppermute x12 -> x0, starting transfers between devices: 35.5 us -> none  [the longest x6 27.8 us: padded_2(): lax.ppermute(tail, axis, [(i, (i + 1) % count) for i in range(ends)])]
    pallas_call x0 -> x1, Pallas kernels: none -> 23.7 us  [local(): pl.pallas_call(functools.partial(body, (nf, nr, fd, rows, cpd, comps)), o...]
    ppermute x12 -> x0, waiting for transfers between devices: 13.3 us -> none  [the longest x6 8.5 us: padded_2(): lax.ppermute(head, axis, [((i + 1) % count, i) for i in range(ends)])]
    div x6 -> x0, other arithmetic: 12.6 us -> none  [the longest x1 9.26 us: temporal(): lax.linalg.tridiagonal_solve(sub_diag, middle, super_diag, values)]
    unnamed x34 -> x4, local copies, waits for them, and re-layouts: 8.98 us -> 2.28 us
    all_to_all x1 -> x0, starting transfers between devices: 3.41 us -> none  [local(): lax.all_to_all(estimate, 'frame', split_axis=2, concat_axis=0, tiled=True)]
  transfers between devices with their start and end apart: 14 -> 0, of which waited for: 9 -> 0; matrix products, arithmetic and copies ran while one was open for 4% -> 0% of each run, Pallas kernels for 0% -> 0%
where the time goes in v1:
time: 26.8 us; the launch traced here: 26.6 us
  Pallas kernels  23.7 us (88%)
  local copies, waits for them, and re-layouts  2.28 us (9%)
  between operations  0.65 us (2%)
    pallas_call x1, Pallas kernels, local(): pl.pallas_call(functools.partial(body, (nf, nr, fd, rows, cpd, comps)), o...  23.7 us
    unnamed x4, local copies, waits for them, and re-layouts  2.28 us

profile of v1, /device:TPU:0, one launch (start us, length us, event | category | flops | bytes accessed | tf_op | source)
XLA Modules:
  0.0 26.6 jit_solution(1989077353450551942)
XLA Ops:
  0.6 23.7 %restore_all.1 = (bf16[16,16,512]{2,1,0:T(8,128)(2,1)}, f32[16,16]{1,0:T(8,128)}) custom-call(f32[4,16,2048]{2,1,0:T(8,128)} %obs_hbm.1, f32[8,5]{1,0:T(8,128)} %kern_ref.1, s32[8]{0:T(128)} %band_ref.1, s32[16,4,256]{2,1,0:T(4,128)} %bitcast.1), custom_call_target="tpu_custom_call" | custom-call | tf_op jit(solution)/shard_map/restore_all/pallas_call | solution.py:370
  24.4 0.0 copy-start
  24.4 1.7 %copy.8 = bf16[16,16,512]{2,1,0:T(8,128)(2,1)} copy(bf16[16,16,512]{2,1,0:T(8,128)(2,1)} %get-tuple-element.4) | data formatting | bytes 524288
  26.0 0.0 copy-done
  26.1 0.6 %copy.9 = f32[16,16]{1,0:T(8,128)} copy(f32[16,16]{1,0:T(8,128)S(1)} %copy-done) | data formatting | bytes 2048
Async XLA Ops:
  24.4 1.7 %copy-start = (f32[16,16]{1,0:T(8,128)S(1)}, f32[16,16]{1,0:T(8,128)}, u32[]{:S(2)}) copy-start(f32[16,16]{1,0:T(8,128)} %get-tuple-element.5) | copy-start | bytes 3076

commit v2 on v1

--- a/solution.py
+++ b/solution.py
@@ -11,6 +11,8 @@
 ITERS = 3
 REACH = 2
 HALO = 2 * REACH * ITERS
+NEAR = 2 * REACH
+FAR = HALO - NEAR
 OWN = 16
 
 SMOOTHING = 1024.0
@@ -28,7 +30,7 @@
 
 
 def body(cfg, obs_hbm, kern_ref, band_ref, masks_hbm, spikes_ref, traces_ref,
-         obs, cur, quo, taps, outm, send, est, masks, wide, wt, rhs, part, gath,
+         obs, far_out, far_in, cur, quo, taps, outm, send, est, masks, wide, wt, rhs, part, gath,
          load_sem, mask_sem, zs, zr, fs, fr, rs, rr):
     nf, nr, fd, rows, cpd, comps = cfg
     ct_n = cpd // TILE
@@ -55,25 +57,29 @@
             load_sem.at[s, ct],
         )
 
-    def up(s):
-        return pltpu.make_async_remote_copy(
-            src_ref=obs.at[s, :, :, OWN : OWN + HALO, :],
-            dst_ref=obs.at[s, :, :, OWN + rows : OWN + rows + HALO, :],
-            send_sem=zs.at[0, s],
-            recv_sem=zr.at[0, s],
-            device_id={"row": r - 1},
-            device_id_type=pl.DeviceIdType.MESH,
-        )
-
-    def down(s):
-        return pltpu.make_async_remote_copy(
-            src_ref=obs.at[s, :, :, OWN + rows - HALO : OWN + rows, :],
-            dst_ref=obs.at[s, :, :, OWN - HALO : OWN, :],
-            send_sem=zs.at[1, s],
-            recv_sem=zr.at[1, s],
-            device_id={"row": r + 1},
-            device_id_type=pl.DeviceIdType.MESH,
-        )
+    near_rows = ((OWN, OWN + rows), (OWN + rows - NEAR, OWN - NEAR))
+    far_rows = ((OWN + NEAR, OWN + rows + NEAR), (OWN + rows - HALO, OWN - HALO))
+
+    def halo(s, way):
+        there = {"row": r - 1 + 2 * way}
+        first, put = near_rows[way]
+        near = pltpu.make_async_remote_copy(
+            src_ref=obs.at[s, :, :, first : first + NEAR, :],
+            dst_ref=obs.at[s, :, :, put : put + NEAR, :],
+            send_sem=zs.at[way, s],
+            recv_sem=zr.at[way, s],
+            device_id=there,
+            device_id_type=pl.DeviceIdType.MESH,
+        )
+        far = pltpu.make_async_remote_copy(
+            src_ref=far_out.at[way, s],
+            dst_ref=far_in.at[way, s],
+            send_sem=zs.at[2 + way, s],
+            recv_sem=zr.at[2 + way, s],
+            device_id=there,
+            device_id_type=pl.DeviceIdType.MESH,
+        )
+        return near, far
 
     def frame_copy(s):
         c = chunk_of(s)
@@ -157,13 +163,16 @@
         for ct in range(ct_n):
             load(s, ct).wait()
 
-        @pl.when(r > 0)
-        def _():
-            up(s).start()
-
-        @pl.when(r < nr - 1)
-        def _():
-            down(s).start()
+        for way in range(2):
+            @pl.when((r > 0) if way == 0 else (r < nr - 1))
+            def _():
+                near, far = halo(s, way)
+                near.start()
+                first = far_rows[way][0]
+                for ff in range(fd):
+                    values = obs[s, ff, :, pl.ds(first, FAR), :].reshape(ct_n * FAR, TILE)
+                    far_out[way, s, ff] = values.astype(jnp.bfloat16)
+                far.start()
 
         return 0
 
@@ -219,13 +228,16 @@
                     cur[ff, :, pl.ds(a, step), :] = value
 
     def wait_halo(s):
-        @pl.when(r > 0)
-        def _():
-            down(s).wait_recv()
-
-        @pl.when(r < nr - 1)
-        def _():
-            up(s).wait_recv()
+        for way in range(2):
+            @pl.when((r < nr - 1) if way == 0 else (r > 0))
+            def _():
+                near, far = halo(s, way)
+                near.wait_recv()
+                far.wait_recv()
+                put = far_rows[way][1]
+                for ff in range(fd):
+                    values = far_in[way, s, ff].astype(jnp.float32)
+                    obs[s, ff, :, pl.ds(put, FAR), :] = values.reshape(ct_n, FAR, TILE)
 
     def remote_chunk(s, _):
         wait_halo(s)
@@ -326,13 +338,12 @@
     lax.fori_loop(0, nf - 1, drain, 0)
 
     def drain_halo(s, _):
-        @pl.when(r > 0)
-        def _():
-            up(s).wait_send()
-
-        @pl.when(r < nr - 1)
-        def _():
-            down(s).wait_send()
+        for way in range(2):
+            @pl.when((r > 0) if way == 0 else (r < nr - 1))
+            def _():
+                near, far = halo(s, way)
+                near.wait_send()
+                far.wait_send()
 
         return 0
 
@@ -367,11 +378,11 @@
     kdev = comps // nd
     f32, bf16 = jnp.float32, jnp.bfloat16
     dma = pltpu.SemaphoreType.DMA
-    return pl.pallas_call(
+    spikes, traces = pl.pallas_call(
         functools.partial(body, (nf, nr, fd, rows, cpd, comps)),
         out_shape=(
-            jax.ShapeDtypeStruct((frames, rows, cpd), bf16),
-            jax.ShapeDtypeStruct((kdev, frames), f32),
+            pltpu.VMEM((frames, rows, cpd), bf16),
+            pltpu.VMEM((kdev, frames), f32),
         ),
         in_specs=[
             pl.BlockSpec(memory_space=pl.ANY),
@@ -385,6 +396,8 @@
         ),
         scratch_shapes=[
             pltpu.VMEM((nf, fd, ct_n, brows, TILE), f32),
+            pltpu.VMEM((2, nf, fd, ct_n * FAR, TILE), bf16),
+            pltpu.VMEM((2, nf, fd, ct_n * FAR, TILE), bf16),
             pltpu.VMEM((fd, ct_n, brows, TILE), f32),
             pltpu.VMEM((fd, ct_n, brows, TILE), f32),
             pltpu.VMEM((5, brows, TILE), f32),
@@ -399,8 +412,8 @@
             pltpu.VMEM((nd, kdev // pack, TILE), f32),
             dma((nf, ct_n)),
             dma,
-            dma((2, nf)),
-            dma((2, nf)),
+            dma((4, nf)),
+            dma((4, nf)),
             dma((nf,)),
             dma((nf,)),
             dma((nd,)),
@@ -409,6 +422,29 @@
         compiler_params=pltpu.CompilerParams(collective_id=0, has_side_effects=True),
         name="restore_all",
     )(observed, kernels, band_kernel, jnp.transpose(masks, (1, 2, 0)))
+    return pl.pallas_call(
+        write_out,
+        out_shape=(
+            jax.ShapeDtypeStruct((frames, rows, cpd), bf16),
+            jax.ShapeDtypeStruct((kdev, frames), f32),
+        ),
+        in_specs=[pl.BlockSpec(memory_space=pltpu.VMEM)] * 2,
+        out_specs=(pl.BlockSpec(memory_space=pl.ANY),) * 2,
+        scratch_shapes=[dma, dma],
+        name="write_out",
+    )(
+        pltpu.with_memory_space_constraint(spikes, pltpu.VMEM),
+        pltpu.with_memory_space_constraint(traces, pltpu.VMEM),
+    )
+
+
+def write_out(spikes_ref, traces_ref, spikes_out, traces_out, spikes_sem, traces_sem):
+    big = pltpu.make_async_copy(spikes_ref, spikes_out, spikes_sem)
+    small = pltpu.make_async_copy(traces_ref, traces_out, traces_sem)
+    big.start()
+    small.start()
+    big.wait()
+    small.wait()
 
 
 def solution(mesh):

time: 26.8 us -> 23.1 us (0.86)
  local copies, waits for them, and re-layouts: 2.28 us -> 0 us
  Pallas kernels: 23.7 us -> 22.3 us
    unnamed x4 -> x0, local copies, waits for them, and re-layouts: 2.28 us -> none
    pallas_call x1, Pallas kernels: 23.7 us -> 21.5 us  [local(): pl.pallas_call(functools.partial(body, (nf, nr, fd, rows, cpd, comps)), o...]
    pallas_call x0 -> x1, Pallas kernels: none -> 0.72 us  [local(): pl.pallas_call(write_out, out_shape=(jax.ShapeDtypeStruct((frames, rows,...]
where the time goes in v2:
time: 23.1 us; the launch traced here: 22.9 us
  Pallas kernels  22.3 us (97%)
  between operations  0.64 us (3%)
    pallas_call x1, Pallas kernels, local(): pl.pallas_call(functools.partial(body, (nf, nr, fd, rows, cpd, comps)), o...  21.5 us
    pallas_call x1, Pallas kernels, local(): pl.pallas_call(write_out, out_shape=(jax.ShapeDtypeStruct((frames, rows,...  0.72 us

profile of v2, /device:TPU:0, one launch (start us, length us, event | category | flops | bytes accessed | tf_op | source)
XLA Modules:
  0.0 22.9 jit_solution(8923215808664247631)
XLA Ops:
  0.6 21.5 %restore_all.1 = (bf16[16,16,512]{2,1,0:T(8,128)(2,1)S(1)}, f32[16,16]{1,0:T(8,128)S(1)}) custom-call(f32[4,16,2048]{2,1,0:T(8,128)} %obs_hbm.1, f32[8,5]{1,0:T(8,128)} %kern_ref.1, s32[8]{0:T(128)} %band_ref.1, s32[16,4,256]{2,1,0:T(4,128)} %bitcast.1), custom_call_target="tpu_custom_call" | custom-call | tf_op jit(solution)/shard_map/restore_all/pallas_call | solution.py:381
  22.2 0.7 %write_out.1 = (bf16[16,16,512]{2,1,0:T(8,128)(2,1)}, f32[16,16]{1,0:T(8,128)}) custom-call(bf16[16,16,512]{2,1,0:T(8,128)(2,1)S(1)} %get-tuple-element.4.spikes_ref, f32[16,16]{1,0:T(8,128)S(1)} %get-tuple-element.5.traces_ref), custom_call_target="tpu_custom_call" | custom-call | tf_op jit(solution)/shard_map/write_out/pallas_call | solution.py:425

commit v3 on v2

--- a/solution.py
+++ b/solution.py
@@ -31,7 +31,7 @@
 
 def body(cfg, obs_hbm, kern_ref, band_ref, masks_hbm, spikes_ref, traces_ref,
          obs, far_out, far_in, cur, quo, taps, outm, send, est, masks, wide, wt, rhs, part, gath,
-         load_sem, mask_sem, zs, zr, fs, fr, rs, rr):
+         load_sem, mask_sem, zs, zr, fs, fr, rs, rr, chain):
     nf, nr, fd, rows, cpd, comps = cfg
     ct_n = cpd // TILE
     frames = fd * nf
@@ -127,15 +127,22 @@
 
     barrier = pltpu.get_barrier_semaphore()
 
+    for way in range(2):
+        @pl.when((r > 0) if way == 0 else (r < nr - 1))
+        def _():
+            pl.semaphore_signal(
+                barrier, inc=1, device_id={"row": r - 1 + 2 * way},
+                device_id_type=pl.DeviceIdType.MESH,
+            )
+
     def greet(off, _):
-        d = (me + off) % nd
         pl.semaphore_signal(
-            barrier, inc=1, device_id={"frame": d // nr, "row": d % nr},
-            device_id_type=pl.DeviceIdType.MESH,
-        )
-        return 0
-
-    lax.fori_loop(1, nd, greet, 0)
+            barrier, inc=1, device_id={"frame": (f + off) % nf},
+            device_id_type=pl.DeviceIdType.MESH,
+        )
+        return 0
+
+    lax.fori_loop(1, nf, greet, 0)
 
     def start_loads(s, _):
         for ct in range(ct_n):
@@ -157,7 +164,8 @@
             taps[j, b * BAND : (b + 1) * BAND, :] = row_taps[j] / total * inside
         outm[b * BAND : (b + 1) * BAND, :] = jnp.full((BAND, TILE), 1.0 - inside, jnp.float32)
 
-    pl.semaphore_wait(barrier, nd - 1)
+    peers = nf - 1 + (r > 0).astype(jnp.int32) + (r < nr - 1).astype(jnp.int32)
+    pl.semaphore_wait(barrier, peers)
 
     def start_halo(s, _):
         for ct in range(ct_n):
@@ -200,6 +208,20 @@
     rhs[...] = jnp.zeros_like(rhs)
     for m in range(pack):
         rhs[m, m * slot + frames : m * slot + frames + 1, :] = jnp.ones((1, TILE), jnp.float32)
+
+    for way in range(2):
+        behind, ahead = ((r > 0), (r < nr - 1)) if way == 0 else ((r < nr - 1), (r > 0))
+
+        @pl.when(behind)
+        def _():
+            pl.semaphore_wait(chain.at[way], 1)
+
+        @pl.when(ahead)
+        def _():
+            pl.semaphore_signal(
+                chain.at[way], inc=1, device_id={"row": r + 1 - 2 * way},
+                device_id_type=pl.DeviceIdType.MESH,
+            )
 
     def restore(s, ff, store):
         for it in range(ITERS):
@@ -418,6 +440,7 @@
             dma((nf,)),
             dma((nd,)),
             dma((nd,)),
+            pltpu.SemaphoreType.REGULAR((2,)),
         ],
         compiler_params=pltpu.CompilerParams(collective_id=0, has_side_effects=True),
         name="restore_all",

time: 23.1 us -> 22.3 us (0.965)
  Pallas kernels: 22.3 us -> 21.4 us
    pallas_call x1, Pallas kernels: 21.5 us -> 20.7 us  [local(): pl.pallas_call(functools.partial(body, (nf, nr, fd, rows, cpd, comps)), o...]
where the time goes in v3:
time: 22.3 us; the launch traced here: 22.1 us
  Pallas kernels  21.4 us (96%)
  between operations  0.64 us (3%)
    pallas_call x1, Pallas kernels, local(): pl.pallas_call(functools.partial(body, (nf, nr, fd, rows, cpd, comps)), o...  20.7 us
    pallas_call x1, Pallas kernels, local(): pl.pallas_call(write_out, out_shape=(jax.ShapeDtypeStruct((frames, rows,...  0.72 us

profile of v3, /device:TPU:0, one launch (start us, length us, event | category | flops | bytes accessed | tf_op | source)
XLA Modules:
  0.0 22.1 jit_solution(1125926791020338280)
XLA Ops:
  0.6 20.7 %restore_all.1 = (bf16[16,16,512]{2,1,0:T(8,128)(2,1)S(1)}, f32[16,16]{1,0:T(8,128)S(1)}) custom-call(f32[4,16,2048]{2,1,0:T(8,128)} %obs_hbm.1, f32[8,5]{1,0:T(8,128)} %kern_ref.1, s32[8]{0:T(128)} %band_ref.1, s32[16,4,256]{2,1,0:T(4,128)} %bitcast.1), custom_call_target="tpu_custom_call" | custom-call | tf_op jit(solution)/shard_map/restore_all/pallas_call | solution.py:403
  21.3 0.7 %write_out.1 = (bf16[16,16,512]{2,1,0:T(8,128)(2,1)}, f32[16,16]{1,0:T(8,128)}) custom-call(bf16[16,16,512]{2,1,0:T(8,128)(2,1)S(1)} %get-tuple-element.4.spikes_ref, f32[16,16]{1,0:T(8,128)S(1)} %get-tuple-element.5.traces_ref), custom_call_target="tpu_custom_call" | custom-call | tf_op jit(solution)/shard_map/write_out/pallas_call | solution.py:448
